TPU v7x, 32 devices: a whole 2x2x4 slice. The times are simulated.
32 devices in a mesh: dp: 8 (over z, core), seq: 4 (over y, x).
Axes of the slice: x: 2, y: 2, z: 4, core: 2. Of those that a mesh axis runs over, the one named last changes fastest.
Arguments:
- inputs: bfloat16 [24, 512, 1024], P('dp', 'seq'), may hold values from -6 to 6
- w_query: bfloat16 [1024, 1024], P('dp'), may hold values from -0.1875 to 0.1875
- w_key: bfloat16 [1024, 1024], P('dp'), may hold values from -0.1875 to 0.1875
- w_value: bfloat16 [1024, 1024], P('dp'), may hold values from -0.1875 to 0.1875
- b_query: bfloat16 [1024], P('dp'), may hold values from -4 to 4
- b_value: bfloat16 [1024], P('dp'), may hold values from -0.75 to 0.75
- w_out: bfloat16 [1024, 1024], P('dp'), may hold values from -2.5 to 2.5
- b_out: bfloat16 [1024], P('dp'), may hold values from -4 to 4
- gain_one: bfloat16 [1024], P('dp'), may hold values from 0.5 to 1.5
- shift_one: bfloat16 [1024], P('dp'), may hold values from -4 to 4
- w_up: bfloat16 [1024, 4096], P('dp'), may hold values from -0.1875 to 0.1875
- b_up: bfloat16 [4096], P('dp'), may hold values from -6 to 6
- w_down: bfloat16 [4096, 1024], P('dp'), may hold values from -0.09375 to 0.09375
- b_down: bfloat16 [1024], P('dp'), may hold values from -4 to 4
- gain_two: bfloat16 [1024], P('dp'), may hold values from 0.5 to 1.5
- shift_two: bfloat16 [1024], P('dp'), may hold values from -4 to 4
- cotangent: bfloat16 [24, 512, 1024], P('dp', 'seq'), may hold values from -6 to 6
Outputs:
- output: bfloat16 [24, 512, 1024], P('dp', 'seq')
- grad_inputs: float32 [24, 512, 1024], P('dp', 'seq')
- grad_w_query: float32 [1024, 1024], P('dp')
- grad_w_key: float32 [1024, 1024], P('dp')
- grad_w_value: float32 [1024, 1024], P('dp')
- grad_b_query: float32 [1024], P('dp')
- grad_b_value: float32 [1024], P('dp')
- grad_w_out: float32 [1024, 1024], P('dp')
- grad_b_out: float32 [1024], P('dp')
- grad_gain_one: float32 [1024], P('dp')
- grad_shift_one: float32 [1024], P('dp')
- grad_w_up: float32 [1024, 4096], P('dp')
- grad_b_up: float32 [4096], P('dp')
- grad_w_down: float32 [4096, 1024], P('dp')
- grad_b_down: float32 [1024], P('dp')
- grad_gain_two: float32 [1024], P('dp')
- grad_shift_two: float32 [1024], P('dp')
All inputs are finite; a program needn't handle non-finite values.
Results may differ from a plain program's by a relative error of at most 0.02.
Values may be sent and summed in bfloat16 or wider, within the bound.
No kernel may reach another device: no remote copies, remote signals or barrier semaphores. Data moves between devices by JAX's collectives and lax.ppermute only.
A program may use at most 192 MiB of HBM per device.

v0:
```python
import jax
import jax.numpy as jnp
from jax import lax
from jax.sharding import PartitionSpec as P

HEAD_DIM = 64
EPSILON = 1e-12


def dot_rows(former, latter):
    return jnp.dot(former, latter, preferred_element_type=jnp.float32)


def dot_left(former, latter):
    return lax.dot_general(
        former, latter, (((0,), (0,)), ((), ())), preferred_element_type=jnp.float32
    )


def dot_right(former, latter):
    return lax.dot_general(
        former, latter, (((1,), (1,)), ((), ())), preferred_element_type=jnp.float32
    )


def normalize(hidden, gain_vec, offset):
    center = hidden - jnp.mean(hidden, -1, keepdims=True)
    spread = jnp.mean(center * center, -1, keepdims=True)
    return center * lax.rsqrt(spread + EPSILON) * gain_vec + offset


def normalize_back(hidden, gain_vec, offset, upstream):
    result, pullback = jax.vjp(normalize, hidden, gain_vec, offset)
    return pullback(upstream)


def activation(hidden):
    return jax.nn.gelu(hidden, approximate=False)


def activation_back(hidden, upstream):
    result, pullback = jax.vjp(activation, hidden)
    return pullback(upstream)[0]


def attend(head_query, head_key, head_value):
    groups, length, columns = head_query.shape
    four_dims = (groups, length, columns // HEAD_DIM, HEAD_DIM)
    factor = HEAD_DIM ** (-0.5)
    scores = (
        jnp.einsum(
            "gqhd,gkhd->ghqk",
            head_query.reshape(four_dims),
            head_key.reshape(four_dims),
            preferred_element_type=jnp.float32,
        )
        * factor
    )
    row_max = jnp.max(scores, -1, keepdims=True)
    exponent = jnp.exp(scores - row_max)
    row_total = jnp.sum(exponent, -1, keepdims=True)
    portions_low = (exponent / row_total).astype(jnp.bfloat16)
    context = jnp.einsum(
        "ghqk,gkhd->gqhd",
        portions_low,
        head_value.reshape(four_dims),
        preferred_element_type=jnp.float32,
    )
    return (
        context.astype(jnp.bfloat16).reshape(groups, length, columns),
        row_max + jnp.log(row_total),
    )


def attend_back(head_query, head_key, head_value, log_total, upstream):
    groups, length, columns = head_query.shape
    four_dims = (groups, length, columns // HEAD_DIM, HEAD_DIM)
    factor = HEAD_DIM ** (-0.5)
    query_four = head_query.reshape(four_dims)
    key_four = head_key.reshape(four_dims)
    upstream_four = upstream.reshape(four_dims)
    scores = (
        jnp.einsum("gqhd,gkhd->ghqk", query_four, key_four, preferred_element_type=jnp.float32)
        * factor
    )
    portions = jnp.exp(scores - log_total)
    portions_low = portions.astype(jnp.bfloat16)
    grad_value = jnp.einsum(
        "ghqk,gqhd->gkhd", portions_low, upstream_four, preferred_element_type=jnp.float32
    )
    grad_portions = jnp.einsum(
        "gqhd,gkhd->ghqk",
        upstream_four,
        head_value.reshape(four_dims),
        preferred_element_type=jnp.float32,
    )
    grad_scores = (
        portions * (grad_portions - jnp.sum(portions * grad_portions, -1, keepdims=True))
    ).astype(jnp.bfloat16)
    grad_query = (
        jnp.einsum("ghqk,gkhd->gqhd", grad_scores, key_four, preferred_element_type=jnp.float32)
        * factor
    )
    grad_key = (
        jnp.einsum("ghqk,gqhd->gkhd", grad_scores, query_four, preferred_element_type=jnp.float32)
        * factor
    )
    three_dims = (groups, length, columns)
    return (
        grad_query.astype(jnp.bfloat16).reshape(three_dims),
        grad_key.astype(jnp.bfloat16).reshape(three_dims),
        grad_value.astype(jnp.bfloat16).reshape(three_dims),
    )


def forward(weights, inputs):
    (
        w_query,
        w_key,
        w_value,
        b_query,
        b_value,
        w_out,
        b_out,
        gain_one,
        shift_one,
        w_up,
        b_up,
        w_down,
        b_down,
        gain_two,
        shift_two,
    ) = weights
    groups, local_len, model_width = inputs.shape
    flat_rows = inputs.reshape(groups * local_len, model_width)
    three_dims = (groups, local_len, model_width)
    queries = (
        (dot_rows(flat_rows, w_query) + b_query.astype(jnp.float32))
        .astype(jnp.bfloat16)
        .reshape(three_dims)
    )
    key_rows = dot_rows(flat_rows, w_key).astype(jnp.bfloat16).reshape(three_dims)
    values = (
        (dot_rows(flat_rows, w_value) + b_value.astype(jnp.float32))
        .astype(jnp.bfloat16)
        .reshape(three_dims)
    )
    head_query, head_key, head_value = (
        lax.all_to_all(queries, "seq", split_axis=2, concat_axis=1, tiled=True),
        lax.all_to_all(key_rows, "seq", split_axis=2, concat_axis=1, tiled=True),
        lax.all_to_all(values, "seq", split_axis=2, concat_axis=1, tiled=True),
    )
    head_context, log_total = attend(head_query, head_key, head_value)
    context = lax.all_to_all(head_context, "seq", split_axis=1, concat_axis=2, tiled=True).reshape(
        groups * local_len, model_width
    )
    first_sum = flat_rows.astype(jnp.float32) + (
        dot_rows(context, w_out) + b_out.astype(jnp.float32)
    )
    normed = normalize(first_sum, gain_one.astype(jnp.float32), shift_one.astype(jnp.float32))
    normed_low = normed.astype(jnp.bfloat16)
    pre_active = dot_rows(normed_low, w_up) + b_up.astype(jnp.float32)
    active = activation(pre_active).astype(jnp.bfloat16)
    second_sum = normed + (dot_rows(active, w_down) + b_down.astype(jnp.float32))
    result = normalize(second_sum, gain_two.astype(jnp.float32), shift_two.astype(jnp.float32))
    stored = (
        flat_rows,
        head_query,
        head_key,
        head_value,
        log_total,
        context,
        first_sum,
        normed_low,
        pre_active,
        active,
        second_sum,
    )
    return (result, stored)


def local(
    inputs,
    w_query,
    w_key,
    w_value,
    b_query,
    b_value,
    w_out,
    b_out,
    gain_one,
    shift_one,
    w_up,
    b_up,
    w_down,
    b_down,
    gain_two,
    shift_two,
    cotangent,
):
    gathered = (
        lax.all_gather(w_query, "dp", axis=0, tiled=True),
        lax.all_gather(w_key, "dp", axis=0, tiled=True),
        lax.all_gather(w_value, "dp", axis=0, tiled=True),
        lax.all_gather(b_query, "dp", axis=0, tiled=True),
        lax.all_gather(b_value, "dp", axis=0, tiled=True),
        lax.all_gather(w_out, "dp", axis=0, tiled=True),
        lax.all_gather(b_out, "dp", axis=0, tiled=True),
        lax.all_gather(gain_one, "dp", axis=0, tiled=True),
        lax.all_gather(shift_one, "dp", axis=0, tiled=True),
        lax.all_gather(w_up, "dp", axis=0, tiled=True),
        lax.all_gather(b_up, "dp", axis=0, tiled=True),
        lax.all_gather(w_down, "dp", axis=0, tiled=True),
        lax.all_gather(b_down, "dp", axis=0, tiled=True),
        lax.all_gather(gain_two, "dp", axis=0, tiled=True),
        lax.all_gather(shift_two, "dp", axis=0, tiled=True),
    )
    result, stored = forward(gathered, inputs)
    output = result.astype(jnp.bfloat16).reshape(inputs.shape)
    weights = (
        lax.all_gather(w_query, "dp", axis=0, tiled=True),
        lax.all_gather(w_key, "dp", axis=0, tiled=True),
        lax.all_gather(w_value, "dp", axis=0, tiled=True),
        lax.all_gather(b_query, "dp", axis=0, tiled=True),
        lax.all_gather(b_value, "dp", axis=0, tiled=True),
        lax.all_gather(w_out, "dp", axis=0, tiled=True),
        lax.all_gather(b_out, "dp", axis=0, tiled=True),
        lax.all_gather(gain_one, "dp", axis=0, tiled=True),
        lax.all_gather(shift_one, "dp", axis=0, tiled=True),
        lax.all_gather(w_up, "dp", axis=0, tiled=True),
        lax.all_gather(b_up, "dp", axis=0, tiled=True),
        lax.all_gather(w_down, "dp", axis=0, tiled=True),
        lax.all_gather(b_down, "dp", axis=0, tiled=True),
        lax.all_gather(gain_two, "dp", axis=0, tiled=True),
        lax.all_gather(shift_two, "dp", axis=0, tiled=True),
    )
    unused, stored = forward(weights, inputs)
    (
        full_query,
        full_key,
        full_value,
        full_bq,
        full_bv,
        full_out,
        full_bo,
        full_gain_one,
        full_shift_one,
        full_up,
        full_bup,
        full_down,
        full_bdown,
        full_gain_two,
        full_shift_two,
    ) = weights
    (
        flat_rows,
        head_query,
        head_key,
        head_value,
        log_total,
        context,
        first_sum,
        normed_low,
        pre_active,
        active,
        second_sum,
    ) = stored
    groups, local_len, model_width = inputs.shape
    upstream = cotangent.reshape(groups * local_len, model_width).astype(jnp.float32)
    grad_second, grad_gain_two, grad_shift_two = normalize_back(
        second_sum, full_gain_two.astype(jnp.float32), full_shift_two.astype(jnp.float32), upstream
    )
    grad_branch_two = grad_second.astype(jnp.bfloat16)
    grad_b_down = jnp.sum(grad_branch_two.astype(jnp.float32), 0)
    grad_w_down = dot_left(active, grad_branch_two)
    grad_pre = activation_back(pre_active, dot_right(grad_branch_two, full_down)).astype(
        jnp.bfloat16
    )
    grad_b_up = jnp.sum(grad_pre.astype(jnp.float32), 0)
    grad_w_up = dot_left(normed_low, grad_pre)
    grad_normed = grad_second + dot_right(grad_pre, full_up)
    grad_first, grad_gain_one, grad_shift_one = normalize_back(
        first_sum,
        full_gain_one.astype(jnp.float32),
        full_shift_one.astype(jnp.float32),
        grad_normed,
    )
    grad_branch_one = grad_first.astype(jnp.bfloat16)
    grad_b_out = jnp.sum(grad_branch_one.astype(jnp.float32), 0)
    grad_w_out = dot_left(context, grad_branch_one)
    grad_context = (
        dot_right(grad_branch_one, full_out)
        .astype(jnp.bfloat16)
        .reshape(groups, local_len, model_width)
    )
    head_grad = lax.all_to_all(grad_context, "seq", split_axis=2, concat_axis=1, tiled=True)
    grad_hq, grad_hk, grad_hv = attend_back(head_query, head_key, head_value, log_total, head_grad)
    grad_queries, grad_keys, grad_values = (
        lax.all_to_all(grad_hq, "seq", split_axis=1, concat_axis=2, tiled=True),
        lax.all_to_all(grad_hk, "seq", split_axis=1, concat_axis=2, tiled=True),
        lax.all_to_all(grad_hv, "seq", split_axis=1, concat_axis=2, tiled=True),
    )
    flat_dims = (groups * local_len, model_width)
    grad_queries = grad_queries.reshape(flat_dims)
    grad_keys = grad_keys.reshape(flat_dims)
    grad_values = grad_values.reshape(flat_dims)
    grad_w_query = dot_left(flat_rows, grad_queries)
    grad_w_key = dot_left(flat_rows, grad_keys)
    grad_w_value = dot_left(flat_rows, grad_values)
    grad_b_query = jnp.sum(grad_queries.astype(jnp.float32), 0)
    grad_b_value = jnp.sum(grad_values.astype(jnp.float32), 0)
    grad_inputs = (
        grad_first
        + dot_right(grad_queries, full_query)
        + dot_right(grad_keys, full_key)
        + dot_right(grad_values, full_value)
    )
    owned_grads = (
        lax.psum_scatter(
            grad_w_query.astype(jnp.bfloat16), "dp", scatter_dimension=0, tiled=True
        ).astype(jnp.float32),
        lax.psum_scatter(
            grad_w_key.astype(jnp.bfloat16), "dp", scatter_dimension=0, tiled=True
        ).astype(jnp.float32),
        lax.psum_scatter(
            grad_w_value.astype(jnp.bfloat16), "dp", scatter_dimension=0, tiled=True
        ).astype(jnp.float32),
        lax.psum_scatter(
            grad_b_query.astype(jnp.bfloat16), "dp", scatter_dimension=0, tiled=True
        ).astype(jnp.float32),
        lax.psum_scatter(
            grad_b_value.astype(jnp.bfloat16), "dp", scatter_dimension=0, tiled=True
        ).astype(jnp.float32),
        lax.psum_scatter(
            grad_w_out.astype(jnp.bfloat16), "dp", scatter_dimension=0, tiled=True
        ).astype(jnp.float32),
        lax.psum_scatter(
            grad_b_out.astype(jnp.bfloat16), "dp", scatter_dimension=0, tiled=True
        ).astype(jnp.float32),
        lax.psum_scatter(
            grad_gain_one.astype(jnp.bfloat16), "dp", scatter_dimension=0, tiled=True
        ).astype(jnp.float32),
        lax.psum_scatter(
            grad_shift_one.astype(jnp.bfloat16), "dp", scatter_dimension=0, tiled=True
        ).astype(jnp.float32),
        lax.psum_scatter(
            grad_w_up.astype(jnp.bfloat16), "dp", scatter_dimension=0, tiled=True
        ).astype(jnp.float32),
        lax.psum_scatter(
            grad_b_up.astype(jnp.bfloat16), "dp", scatter_dimension=0, tiled=True
        ).astype(jnp.float32),
        lax.psum_scatter(
            grad_w_down.astype(jnp.bfloat16), "dp", scatter_dimension=0, tiled=True
        ).astype(jnp.float32),
        lax.psum_scatter(
            grad_b_down.astype(jnp.bfloat16), "dp", scatter_dimension=0, tiled=True
        ).astype(jnp.float32),
        lax.psum_scatter(
            grad_gain_two.astype(jnp.bfloat16), "dp", scatter_dimension=0, tiled=True
        ).astype(jnp.float32),
        lax.psum_scatter(
            grad_shift_two.astype(jnp.bfloat16), "dp", scatter_dimension=0, tiled=True
        ).astype(jnp.float32),
    )
    summed = (
        lax.psum(owned_grads[0].astype(jnp.bfloat16), "seq").astype(jnp.float32),
        lax.psum(owned_grads[1].astype(jnp.bfloat16), "seq").astype(jnp.float32),
        lax.psum(owned_grads[2].astype(jnp.bfloat16), "seq").astype(jnp.float32),
        lax.psum(owned_grads[3].astype(jnp.bfloat16), "seq").astype(jnp.float32),
        lax.psum(owned_grads[4].astype(jnp.bfloat16), "seq").astype(jnp.float32),
        lax.psum(owned_grads[5].astype(jnp.bfloat16), "seq").astype(jnp.float32),
        lax.psum(owned_grads[6].astype(jnp.bfloat16), "seq").astype(jnp.float32),
        lax.psum(owned_grads[7].astype(jnp.bfloat16), "seq").astype(jnp.float32),
        lax.psum(owned_grads[8].astype(jnp.bfloat16), "seq").astype(jnp.float32),
        lax.psum(owned_grads[9].astype(jnp.bfloat16), "seq").astype(jnp.float32),
        lax.psum(owned_grads[10].astype(jnp.bfloat16), "seq").astype(jnp.float32),
        lax.psum(owned_grads[11].astype(jnp.bfloat16), "seq").astype(jnp.float32),
        lax.psum(owned_grads[12].astype(jnp.bfloat16), "seq").astype(jnp.float32),
        lax.psum(owned_grads[13].astype(jnp.bfloat16), "seq").astype(jnp.float32),
        lax.psum(owned_grads[14].astype(jnp.bfloat16), "seq").astype(jnp.float32),
    )
    return (output, grad_inputs.reshape(inputs.shape)) + tuple(summed)


def solution(mesh):
    placed = (
        P("dp", "seq", None),
        P("dp", None),
        P("dp", None),
        P("dp", None),
        P("dp"),
        P("dp"),
        P("dp", None),
        P("dp"),
        P("dp"),
        P("dp"),
        P("dp", None),
        P("dp"),
        P("dp", None),
        P("dp"),
        P("dp"),
        P("dp"),
        P("dp", "seq", None),
    )
    return jax.shard_map(
        local,
        mesh=mesh,
        in_specs=placed,
        out_specs=(
            P("dp", "seq", None),
            P("dp", "seq", None),
            P("dp", None),
            P("dp", None),
            P("dp", None),
            P("dp"),
            P("dp"),
            P("dp", None),
            P("dp"),
            P("dp"),
            P("dp"),
            P("dp", None),
            P("dp"),
            P("dp", None),
            P("dp"),
            P("dp"),
            P("dp"),
        ),
        check_vma=False,
    )
```

profile of v0, /device:TPU:0, one launch (start us, length us, event | category | flops | bytes accessed | tf_op | source)
XLA Modules:
  0.0 830.0 jit_solution(2075484790764947876)
XLA Ops:
  11.2 13.5 %all-gather = bf16[8,1,128]{2,1,0:T(2,128)(2,1)S(1)} all-gather(bf16[1,1,128]{2,1,0:T(2,128)(2,1)S(1)} %bitcast.204), channel_id=1, replica_groups=mesh['dp'=8,'seq'=4] {'dp'}, dimensions={0}, use_global_device_ids=true | all-gather | bytes 2304 | tf_op jit(solution)/shard_map/all_gather | solution.py:206
  24.7 16.8 %all-gather.16.cloned.1.call-done = bf16[1024,1024]{1,0:T(8,128)(2,1)} async-done(((bf16[128,1024]{1,0:T(8,128)(2,1)}), bf16[1024,1024]{1,0:T(8,128)(2,1)}) %all-gather.16.cloned.1.call-update) | async-done | bytes 2097168 | tf_op jit(solution)/shard_map/all_gather | solution.py:204
  45.5 3.6 all-to-all-start
  49.2 10.3 %all-gather.1 = bf16[8,1,128]{2,1,0:T(2,128)(2,1)S(1)} all-gather(bf16[1,1,128]{2,1,0:T(2,128)(2,1)S(1)} %bitcast.205), channel_id=1, replica_groups=mesh['dp'=8,'seq'=4] {'dp'}, dimensions={0}, use_global_device_ids=true | all-gather | bytes 2304 | tf_op jit(solution)/shard_map/all_gather | solution.py:205
  59.5 12.3 %all-gather.18.cloned.1.call-done = bf16[1024,1024]{1,0:T(8,128)(2,1)} async-done(((bf16[128,1024]{1,0:T(8,128)(2,1)}), bf16[1024,1024]{1,0:T(8,128)(2,1)}) %all-gather.18.cloned.1.call-update) | async-done | bytes 2097168 | tf_op jit(solution)/shard_map/all_gather | solution.py:202
  75.8 3.6 all-to-all-start.1
  79.4 22.6 %all-gather.20.cloned.1.call-done = bf16[1024,1024]{1,0:T(8,128)(2,1)} async-done(((bf16[128,1024]{1,0:T(8,128)(2,1)}), bf16[1024,1024]{1,0:T(8,128)(2,1)}) %all-gather.20.cloned.1.call-update) | async-done | bytes 2097168 | tf_op jit(solution)/shard_map/all_gather | solution.py:203
  102.0 2.8 convolution_convert_fusion.4
  106.2 3.9 all-to-all-start.2
  115.1 9.1 %all-to-all-done.2 = bf16[3,128,1024]{1,0,2:T(4,128)(2,1)S(1)} async-done(((bf16[3,128,1024]{1,0,2:T(4,128)(2,1)}), bf16[3,128,1024]{1,0,2:T(4,128)(2,1)S(1)}, u32[]{:S(2)}, u32[]{:S(2)}) %all-to-all-start.2) | async-done | bytes 786464 | tf_op jit(solution)/shard_map/all_to_all | solution.py:150
  131.7 2.8 fusion.20
  136.0 3.5 all-to-all-start.3
  139.5 10.5 %all-gather.6 = bf16[8,1,128]{2,1,0:T(2,128)(2,1)S(1)} all-gather(bf16[1,1,128]{2,1,0:T(2,128)(2,1)S(1)} %bitcast.206), channel_id=1, replica_groups=mesh['dp'=8,'seq'=4] {'dp'}, dimensions={0}, use_global_device_ids=true | all-gather | bytes 2304 | tf_op jit(solution)/shard_map/all_gather | solution.py:214
  150.0 12.9 %all-gather.5 = bf16[8,1,512]{2,1,0:T(2,128)(2,1)S(1)} all-gather(bf16[1,1,512]{2,1,0:T(2,128)(2,1)S(1)} %reshape.226), channel_id=1, replica_groups=mesh['dp'=8,'seq'=4] {'dp'}, dimensions={0}, use_global_device_ids=true | all-gather | bytes 9216 | tf_op jit(solution)/shard_map/all_gather | solution.py:212
  163.0 9.6 %all-gather.2 = bf16[8,1,128]{2,1,0:T(2,128)(2,1)S(1)} all-gather(bf16[1,1,128]{2,1,0:T(2,128)(2,1)S(1)} %bitcast.207), channel_id=1, replica_groups=mesh['dp'=8,'seq'=4] {'dp'}, dimensions={0}, use_global_device_ids=true | all-gather | bytes 2304 | tf_op jit(solution)/shard_map/all_gather | solution.py:208
  172.5 11.3 %all-gather.4 = bf16[8,1,128]{2,1,0:T(2,128)(2,1)S(1)} all-gather(bf16[1,1,128]{2,1,0:T(2,128)(2,1)S(1)} %bitcast.208), channel_id=1, replica_groups=mesh['dp'=8,'seq'=4] {'dp'}, dimensions={0}, use_global_device_ids=true | all-gather | bytes 2304 | tf_op jit(solution)/shard_map/all_gather | solution.py:210
  183.8 8.8 %all-gather.3 = bf16[8,1,128]{2,1,0:T(2,128)(2,1)S(1)} all-gather(bf16[1,1,128]{2,1,0:T(2,128)(2,1)S(1)} %bitcast.209), channel_id=1, replica_groups=mesh['dp'=8,'seq'=4] {'dp'}, dimensions={0}, use_global_device_ids=true | all-gather | bytes 2304 | tf_op jit(solution)/shard_map/all_gather | solution.py:209
  192.6 10.0 %all-gather.7 = bf16[8,1,128]{2,1,0:T(2,128)(2,1)S(1)} all-gather(bf16[1,1,128]{2,1,0:T(2,128)(2,1)S(1)} %bitcast.210), channel_id=1, replica_groups=mesh['dp'=8,'seq'=4] {'dp'}, dimensions={0}, use_global_device_ids=true | all-gather | bytes 2304 | tf_op jit(solution)/shard_map/all_gather | solution.py:215
  202.6 10.0 %all-gather.8 = bf16[8,1,128]{2,1,0:T(2,128)(2,1)S(1)} all-gather(bf16[1,1,128]{2,1,0:T(2,128)(2,1)S(1)} %bitcast.211), channel_id=1, replica_groups=mesh['dp'=8,'seq'=4] {'dp'}, dimensions={0}, use_global_device_ids=true | all-gather | bytes 2304 | tf_op jit(solution)/shard_map/all_gather | solution.py:216
  213.6 3.2 fusion.34
  217.1 20.7 %multiply_convert_fusion.1 = (bf16[384,4096]{1,0:T(8,128)(2,1)}, f32[384,4096]{1,0:T(8,128)}, f32[384,4096]{1,0:T(8,128)}) fusion(f32[4096]{0:T(1024)S(1)} %bitcast.187, bf16[1024,4096]{1,0:T(8,128)(2,1)} %all-gather.24.cloned.1.call-done, f32[384,1024]{1,0:T(8,128)S(1)} %get-tuple-element.130, f32[1024]{0:T(1024)S(1)} %bitcast.197, ...), kind=kOutput, calls=%fused_computation.15 | convolution fusion | flops 3327000576 | bytes 25717760 | tf_op jit(solution)/shard_map/dot_general | solution.py:11
  237.8 59.7 %all-gather.26.cloned.1.call-done = bf16[4096,1024]{1,0:T(8,128)(2,1)} async-done(((bf16[512,1024]{1,0:T(8,128)(2,1)}), bf16[4096,1024]{1,0:T(8,128)(2,1)}) %all-gather.26.cloned.1.call-update) | async-done | bytes 8388624 | tf_op jit(solution)/shard_map/all_gather | solution.py:213
  297.5 7.0 fusion.35
  307.3 13.3 %fusion.29 = (bf16[4096]{0:T(1024)(128)(2,1)S(1)}, bf16[384,4096]{1,0:T(8,128)(2,1)S(1)}) fusion(f32[384,4096]{1,0:T(8,128)} %get-tuple-element.125, f32[384,4096]{1,0:T(8,128)} %get-tuple-element.131, bf16[384,1024]{1,0:T(8,128)(2,1)S(1)} %get-tuple-element.115, bf16[4096,1024]{1,0:T(8,128)(2,1)} %all-gather.26.cloned.1.call-done), kind=kOutput, calls=%fused_computation.83 | convolution fusion | flops 3244814336 | bytes 24911872 | tf_op jit(solution)/shard_map/dot_general | solution.py:21
  320.6 3.9 multiply_reduce_fusion.2
  330.3 3.7 all-to-all-start.4
  334.0 14.1 %all-to-all-done.4 = bf16[3,128,1024]{1,0,2:T(4,128)(2,1)S(1)} async-done(((bf16[3,128,1024]{1,0,2:T(4,128)(2,1)}), bf16[3,128,1024]{1,0,2:T(4,128)(2,1)S(1)}, u32[]{:S(2)}, u32[]{:S(2)}) %all-to-all-start.4) | async-done | bytes 786464 | tf_op jit(solution)/shard_map/all_to_all | solution.py:296
  351.4 6.5 multiply_reduce_fusion
  357.9 6.8 multiply_convert_fusion
  369.9 17.6 %all_to_all.140 = bf16[3,512,256]{2,0,1:T(4,128)(2,1)S(1)} all-to-all(bf16[3,512,256]{2,0,1:T(4,128)(2,1)} %copy.88), channel_id=1, replica_groups=mesh['dp'=8,'seq'=4] {'seq'}, dimensions={1} | all-to-all | bytes 1572864 | tf_op jit(solution)/shard_map/all_to_all | solution.py:299
  392.9 3.9 copy.106
  396.9 5.7 multiply_convert_fusion.2
  404.9 16.0 %all_to_all.141 = bf16[3,512,256]{2,0,1:T(4,128)(2,1)S(1)} all-to-all(bf16[3,512,256]{2,0,1:T(4,128)(2,1)} %copy.92), channel_id=1, replica_groups=mesh['dp'=8,'seq'=4] {'seq'}, dimensions={1} | all-to-all | bytes 1572864 | tf_op jit(solution)/shard_map/all_to_all | solution.py:300
  424.4 4.0 copy.108
  428.5 7.8 fusion.17
  437.9 13.4 %all_to_all.142 = bf16[3,512,256]{2,0,1:T(4,128)(2,1)S(1)} all-to-all(bf16[3,512,256]{2,0,1:T(4,128)(2,1)S(1)} %copy.96), channel_id=1, replica_groups=mesh['dp'=8,'seq'=4] {'seq'}, dimensions={1} | all-to-all | bytes 1572864 | tf_op jit(solution)/shard_map/all_to_all | solution.py:301
  455.7 4.0 copy.110
  460.1 3.8 convolution_convert_fusion.2
  463.9 10.4 %convolution_convert_fusion.1 = bf16[1024,4096]{1,0:T(8,128)(2,1)} fusion(bf16[384,4096]{1,0:T(8,128)(2,1)} %copy-done.38, f32[384,1024]{1,0:T(8,128)} %copy-done.7, f32[1024]{0:T(1024)S(1)} %bitcast.199, f32[1024]{0:T(1024)S(1)} %bitcast.192, f32[384]{0:T(512)S(1)} %fusion.22, f32[384]{0:T(512)S(1)} %broadcast_multiply_fusion.1), kind=kOutput, calls=%fused_computation.10 | convolution fusion | flops 3227385856 | bytes 13118464 | tf_op jit(solution)/shard_map/dot_general | solution.py:15
  475.4 8.7 %convolution_convert_fusion = bf16[4096,1024]{1,0:T(8,128)(2,1)} fusion(bf16[384,4096]{1,0:T(8,128)(2,1)} %get-tuple-element.124, bf16[384,1024]{1,0:T(8,128)(2,1)S(1)} %copy-done.20), kind=kOutput, calls=%fused_computation.9 | convolution fusion | flops 3225419776 | bytes 12320768 | tf_op jit(solution)/shard_map/dot_general | solution.py:15
  487.9 15.7 %reduce-scatter.23.cloned.1.call-done = bf16[128,1024]{1,0:T(8,128)(2,1)} async-done(((bf16[1024,1024]{1,0:T(8,128)(2,1)}), bf16[128,1024]{1,0:T(8,128)(2,1)}) %reduce-scatter.23.cloned.1.call-update) | async-done | bytes 262160
  505.4 35.2 %reduce-scatter.13.cloned.1.call-done = bf16[128,1024]{1,0:T(8,128)(2,1)} async-done(((bf16[1024,1024]{1,0:T(8,128)(2,1)}), bf16[128,1024]{1,0:T(8,128)(2,1)}) %reduce-scatter.13.cloned.1.call-update) | async-done | bytes 262160 | tf_op jit(solution)/shard_map/reduce_scatter | solution.py:334
  540.6 90.6 %reduce-scatter.15.cloned.1.call-done = bf16[128,4096]{1,0:T(8,128)(2,1)} async-done(((bf16[1024,4096]{1,0:T(8,128)(2,1)}), bf16[128,4096]{1,0:T(8,128)(2,1)}) %reduce-scatter.15.cloned.1.call-update) | async-done | bytes 1048592 | tf_op jit(solution)/shard_map/reduce_scatter | solution.py:346
  631.2 90.1 %reduce-scatter.17.cloned.1.call-done = bf16[512,1024]{1,0:T(8,128)(2,1)} async-done(((bf16[4096,1024]{1,0:T(8,128)(2,1)}), bf16[512,1024]{1,0:T(8,128)(2,1)}) %reduce-scatter.17.cloned.1.call-update) | async-done | bytes 1048592 | tf_op jit(solution)/shard_map/reduce_scatter | solution.py:352
  724.8 26.1 %all-reduce.9 = (bf16[1024]{0:T(1024)(128)(2,1)S(1)}, bf16[1024]{0:T(1024)(128)(2,1)S(1)}, bf16[1024]{0:T(1024)(128)(2,1)S(1)}, bf16[1024]{0:T(1024)(128)(2,1)S(...) all-reduce(bf16[1024]{0:T(1024)(128)(2,1)S(1)} %bitcast.195, ...), channel_id=5, replica_groups=mesh['dp'=8,'seq'=4] {'dp'}, use_global_device_ids=true, to_apply=%region_18.0.clone | all-reduce | flops 12288 | bytes 49152
  751.6 10.5 %all-reduce.10 = (bf16[128]{0:T(256)(128)(2,1)S(1)}, bf16[128]{0:T(256)(128)(2,1)S(1)}, bf16[128]{0:T(256)(128)(2,1)S(1)}, bf16[128]{0:T(256)(128)(2,1)S(1)}, bf...) all-reduce(bf16[128]{0:T(256)(128)(2,1)S(1)} %dynamic-slice.1, ...), channel_id=1, replica_groups=mesh['dp'=8,'seq'=4] {'seq'}, use_global_device_ids=true, to_apply=%region_19.0 | all-reduce | flops 1536 | bytes 6144 | tf_op jit(solution)/shard_map/psum | solution.py:369
  766.9 2.9 fusion.37
  774.0 38.3 %all-reduce.14.cloned.1.call-done = (bf16[128,1024]{0,1:T(8,128)(2,1)}, bf16[128,1024]{0,1:T(8,128)(2,1)}, bf16[128,1024]{0,1:T(8,128)(2,1)}, bf16[128,1024]{1,0...) async-done(((bf16[128,1024]{0,1:T(8,128)(2,1)}, bf16[128,1024]{0,1:T(8,128)(2,1)}, bf16[128,1024]{0,1:T(8,128)(2,1)}, bf16[128,1024]{1,0:T(8,128)(2,1)}, ...) | async-done | bytes 3145744 | tf_op jit(solution)/shard_map/psum | solution.py:366
  (214 shorter events, 92.0 us)
Async XLA Ops:
  7.2 4.0 copy-start.23
  7.2 34.3 %copy-start.33 = (bf16[3,128,1024]{2,1,0:T(8,128)(2,1)S(1)}, bf16[3,128,1024]{2,1,0:T(8,128)(2,1)}, u32[]{:S(2)}) copy-start(bf16[3,128,1024]{2,1,0:T(8,128)(2,1)} %param.17) | copy-start | bytes 2359300
  7.2 34.3 %all-gather.16.cloned.1.call-start = ((), (), s32[]{:S(2)}) async-start(), calls=%async_computation.14 | async-start | bytes 2359296 | tf_op jit(solution)/shard_map/all_gather | solution.py:204
  7.9 63.8 %all-gather.18.cloned.1.call-start = ((), (), s32[]{:S(2)}) async-start(), calls=%async_computation.15 | async-start | bytes 2359296 | tf_op jit(solution)/shard_map/all_gather | solution.py:202
  8.7 93.3 %all-gather.20.cloned.1.call-start = ((), (), s32[]{:S(2)}) async-start(), calls=%async_computation.16 | async-start | bytes 2359296 | tf_op jit(solution)/shard_map/all_gather | solution.py:203
  9.4 204.1 %all-gather.22.cloned.1.call-start = ((), (), s32[]{:S(2)}) async-start(), calls=%async_computation.17 | async-start | bytes 2359296 | tf_op jit(solution)/shard_map/all_gather | solution.py:207
  10.0 207.1 %all-gather.24.cloned.1.call-start = ((), (), s32[]{:S(2)}) async-start(), calls=%async_computation.18 | async-start | bytes 9437184 | tf_op jit(solution)/shard_map/all_gather | solution.py:211
  10.6 286.9 %all-gather.26.cloned.1.call-start = ((), (), s32[]{:S(2)}) async-start(), calls=%async_computation.19 | async-start | bytes 9437184 | tf_op jit(solution)/shard_map/all_gather | solution.py:213
  44.1 5.1 copy-start.24
  45.5 30.2 %all-to-all-start = ((bf16[3,128,1024]{1,0,2:T(4,128)(2,1)}), bf16[3,128,1024]{1,0,2:T(4,128)(2,1)S(1)}, u32[]{:S(2)}, u32[]{:S(2)}) async-start(bf16[3,128,1024]{1,0,2:T(4,128)(2,1)} %copy.75), calls=%async_computation | async-start | bytes 2097152 | tf_op jit(solution)/shard_map/all_to_all | solution.py:151
  75.8 30.5 %all-to-all-start.1 = ((bf16[3,128,1024]{1,0,2:T(4,128)(2,1)}), bf16[3,128,1024]{1,0,2:T(4,128)(2,1)S(1)}, u32[]{:S(2)}, u32[]{:S(2)}) async-start(bf16[3,128,1024]{1,0,2:T(4,128)(2,1)} %copy.77), calls=%async_computation.1 | async-start | bytes 2097152 | tf_op jit(solution)/shard_map/all_to_all | solution.py:149
  106.2 18.0 %all-to-all-start.2 = ((bf16[3,128,1024]{1,0,2:T(4,128)(2,1)}), bf16[3,128,1024]{1,0,2:T(4,128)(2,1)S(1)}, u32[]{:S(2)}, u32[]{:S(2)}) async-start(bf16[3,128,1024]{1,0,2:T(4,128)(2,1)} %copy.79), calls=%async_computation.2 | async-start | bytes 2097152 | tf_op jit(solution)/shard_map/all_to_all | solution.py:150
  127.2 4.5 copy-start
  127.2 4.5 copy-start.8
  134.5 5.0 copy-start.25
  134.5 15.5 %copy-start.22 = (bf16[512]{0:T(512)(128)(2,1)S(1)}, bf16[512]{0:T(512)(128)(2,1)}, u32[]{:S(2)}) copy-start(bf16[512]{0:T(512)(128)(2,1)} %param.28) | copy-start | bytes 3076
  134.6 28.4 %copy-start.26 = (bf16[128]{0:T(256)(128)(2,1)S(1)}, bf16[128]{0:T(256)(128)(2,1)}, u32[]{:S(2)}) copy-start(bf16[128]{0:T(256)(128)(2,1)} %param.24) | copy-start | bytes 772
  134.6 38.0 %copy-start.27 = (bf16[128]{0:T(256)(128)(2,1)S(1)}, bf16[128]{0:T(256)(128)(2,1)}, u32[]{:S(2)}) copy-start(bf16[128]{0:T(256)(128)(2,1)} %param.26) | copy-start | bytes 772
  134.6 49.2 %copy-start.28 = (bf16[128]{0:T(256)(128)(2,1)S(1)}, bf16[128]{0:T(256)(128)(2,1)}, u32[]{:S(2)}) copy-start(bf16[128]{0:T(256)(128)(2,1)} %param.25) | copy-start | bytes 772
  134.6 58.0 %copy-start.29 = (bf16[128]{0:T(256)(128)(2,1)S(1)}, bf16[128]{0:T(256)(128)(2,1)}, u32[]{:S(2)}) copy-start(bf16[128]{0:T(256)(128)(2,1)} %param.31) | copy-start | bytes 772
  134.6 68.0 %copy-start.30 = (bf16[128]{0:T(256)(128)(2,1)S(1)}, bf16[128]{0:T(256)(128)(2,1)}, u32[]{:S(2)}) copy-start(bf16[128]{0:T(256)(128)(2,1)} %param.32) | copy-start | bytes 772
  136.0 76.6 %all-to-all-start.3 = ((bf16[3,512,256]{2,0,1:T(4,128)(2,1)}), bf16[3,512,256]{2,0,1:T(4,128)(2,1)S(1)}, u32[]{:S(2)}, u32[]{:S(2)}) async-start(bf16[3,512,256]{2,0,1:T(4,128)(2,1)} %copy.82), calls=%async_computation.3 | async-start | bytes 2097152 | tf_op jit(solution)/shard_map/all_to_all | solution.py:154
  216.7 103.9 %copy-start.7 = (f32[384,1024]{1,0:T(8,128)}, f32[384,1024]{1,0:T(8,128)S(1)}, u32[]{:S(2)}) copy-start(f32[384,1024]{1,0:T(8,128)S(1)} %get-tuple-element.130) | copy-start | bytes 4718596
  297.5 7.4 copy-start.4
  305.5 15.1 %slice-start = ((s8[8388608]{0:T(1024)(128)(4,1)}), s8[4194304]{0:T(1024)(128)(4,1)S(1)}, s32[]{:S(2)}) async-start(s8[8388608]{0:T(1024)(128)(4,1)} %bitcast.212), calls=%async_computation.27 | async-start | bytes 8388608
  307.3 13.3 %copy-start.19 = (bf16[384,1024]{1,0:T(8,128)(2,1)}, bf16[384,1024]{1,0:T(8,128)(2,1)S(1)}, u32[]{:S(2)}) copy-start(bf16[384,1024]{1,0:T(8,128)(2,1)S(1)} %get-tuple-element.115) | copy-start | bytes 2359300
  307.3 13.3 %slice-start.1 = ((s8[8388608]{0:T(1024)(128)(4,1)}), s8[4194304]{0:T(1024)(128)(4,1)S(1)}, s32[]{:S(2)}) async-start(s8[8388608]{0:T(1024)(128)(4,1)} %bitcast.212), calls=%async_computation.28 | async-start | bytes 8388608
  320.6 4.0 copy-start.38
  324.6 3.2 copy-start.32
  330.3 17.8 %all-to-all-start.4 = ((bf16[3,128,1024]{1,0,2:T(4,128)(2,1)}), bf16[3,128,1024]{1,0,2:T(4,128)(2,1)S(1)}, u32[]{:S(2)}, u32[]{:S(2)}) async-start(bf16[3,128,1024]{1,0,2:T(4,128)(2,1)} %copy.85), calls=%async_computation.4 | async-start | bytes 2097152 | tf_op jit(solution)/shard_map/all_to_all | solution.py:296
  333.9 150.3 %reduce-scatter.19.cloned.1.call-start = ((), (), s32[]{:S(2)}) async-start(), calls=%async_computation.23 | async-start | bytes 2359296
  357.9 6.8 copy-start.6
  369.9 20.4 %copy-start.34 = (bf16[3,128,1024]{2,1,0:T(8,128)(2,1)S(1)}, bf16[3,128,1024]{2,1,0:T(8,128)(2,1)}, u32[]{:S(2)}) copy-start(bf16[3,128,1024]{2,1,0:T(8,128)(2,1)} %param.17) | copy-start | bytes 2359300
  396.9 89.2 %reduce-scatter.21.cloned.1.call-start = ((), (), s32[]{:S(2)}) async-start(), calls=%async_computation.24 | async-start | bytes 2359296
  404.9 16.9 %copy-start.35 = (bf16[3,128,1024]{2,1,0:T(8,128)(2,1)S(1)}, bf16[3,128,1024]{2,1,0:T(8,128)(2,1)}, u32[]{:S(2)}) copy-start(bf16[3,128,1024]{2,1,0:T(8,128)(2,1)} %param.17) | copy-start | bytes 2359300
  428.4 75.2 %reduce-scatter.23.cloned.1.call-start = ((), (), s32[]{:S(2)}) async-start(), calls=%async_computation.25 | async-start | bytes 2359296
  437.9 15.2 %copy-start.36 = (bf16[3,128,1024]{2,1,0:T(8,128)(2,1)S(1)}, bf16[3,128,1024]{2,1,0:T(8,128)(2,1)}, u32[]{:S(2)}) copy-start(bf16[3,128,1024]{2,1,0:T(8,128)(2,1)} %param.17) | copy-start | bytes 2359300
  455.7 4.3 copy-start.18
  459.8 80.9 %reduce-scatter.13.cloned.1.call-start = ((), (), s32[]{:S(2)}) async-start(), calls=%async_computation.20 | async-start | bytes 2359296 | tf_op jit(solution)/shard_map/reduce_scatter | solution.py:334
  463.9 167.3 %reduce-scatter.15.cloned.1.call-start = ((), (), s32[]{:S(2)}) async-start(), calls=%async_computation.21 | async-start | bytes 9437184 | tf_op jit(solution)/shard_map/reduce_scatter | solution.py:346
  474.3 247.0 %reduce-scatter.17.cloned.1.call-start = ((), (), s32[]{:S(2)}) async-start(), calls=%async_computation.22 | async-start | bytes 9437184 | tf_op jit(solution)/shard_map/reduce_scatter | solution.py:352
  484.1 238.5 %copy-start.37 = (u32[32]{0:T(128)S(1)}, u32[32]{0:T(128)}, u32[]{:S(2)}) copy-start(u32[32]{0:T(128)} %constant.93) | copy-start | bytes 388
  484.1 240.4 %copy-start.3 = (bf16[3,512,256]{2,1,0:T(8,128)(2,1)S(1)}, bf16[3,512,256]{2,1,0:T(8,128)(2,1)}, u32[]{:S(2)}) copy-start(bf16[3,512,256]{2,1,0:T(8,128)(2,1)} %copy-done.2) | copy-start | bytes 2359300
  484.1 328.1 %all-reduce.14.cloned.1.call-start = ((), (), s32[]{:S(2)}) async-start(), calls=%async_computation.26 | async-start | bytes 6291456 | tf_op jit(solution)/shard_map/psum | solution.py:366
  724.7 45.1 %copy-start.15 = (bf16[48,8,4,256]{3,1,2,0:T(8,128)(2,1)S(1)}, bf16[48,8,4,256]{3,1,2,0:T(8,128)(2,1)}, u32[]{:S(2)}) copy-start(bf16[48,8,4,256]{3,1,2,0:T(8,128)(2,1)} %copy-done.14) | copy-start | bytes 2359300
  762.2 7.6 copy-start.31
  812.2 7.6 copy-start.13
  812.3 9.1 %copy-start.12 = (bf16[512,1024]{1,0:T(8,128)(2,1)S(1)}, bf16[512,1024]{1,0:T(8,128)(2,1)}, u32[]{:S(2)}) copy-start(bf16[512,1024]{1,0:T(8,128)(2,1)} %get-tuple-element.113) | copy-start | bytes 3145732
  (11 other events, 18.4 us)
Sparse Core Ops, SparseCore 0:
  9.6 31.7 all-gather.15
  43.1 28.6 all-gather.17
  73.3 28.5 all-gather.19
  103.4 28.5 all-gather.21
  133.5 81.7 all-gather.23
  216.7 80.6 all-gather.25
  397.0 32.8 reduce-scatter.18
  432.2 34.4 reduce-scatter.20
  469.0 34.5 reduce-scatter.22
  506.3 34.2 reduce-scatter.12
  542.9 88.2 reduce-scatter.14
  633.4 87.9 reduce-scatter.16
  725.6 86.5 all-reduce.13
where the time goes:
time: 835 us; the launch traced here: 830 us
  waiting for transfers between devices  408 us (49%)
  blocking collectives  180 us (22%)
  matrix products  121 us (14%)
  local copies, waits for them, and re-layouts  59 us (7%)
  other arithmetic  25.5 us (3%)
  starting transfers between devices  19.1 us (2%)
  between operations  16.5 us (2%)
    reduce_scatter x1, waiting for transfers between devices, local(): lax.psum_scatter(grad_w_up.astype(jnp.bfloat16), 'dp', scatter_dimension=...  90.6 us
    reduce_scatter x1, waiting for transfers between devices, local(): lax.psum_scatter(grad_w_down.astype(jnp.bfloat16), 'dp', scatter_dimensio...  90.1 us
    all_gather x1, waiting for transfers between devices, local(): lax.all_gather(w_down, 'dp', axis=0, tiled=True)  59.7 us
    dot_general x6, matrix products, dot_rows(): return jnp.dot(former, latter, preferred_element_type=jnp.float32)  38.9 us
    psum x1, waiting for transfers between devices, local(): lax.psum(owned_grads[0].astype(jnp.bfloat16), 'seq').astype(jnp.float32)  38.3 us
    reduce_scatter x1, waiting for transfers between devices, local(): lax.psum_scatter(grad_w_out.astype(jnp.bfloat16), 'dp', scatter_dimension...  35.2 us
    unnamed x108, local copies, waits for them, and re-layouts  33.4 us
    dot_general x6, matrix products, dot_left(): lax.dot_general(former, latter, (((0,), (0,)), ((), ())), preferred_eleme...  30.7 us
  transfers between devices with their start and end apart: 18, of which 11 were waited for; matrix products, arithmetic and copies ran while one was open for 15% of the time, Pallas kernels for 0%

commit v1 on v0

--- a/solution.py
+++ b/solution.py
@@ -5,6 +5,27 @@
 
 HEAD_DIM = 64
 EPSILON = 1e-12
+
+
+def joined_along(tiles, dim):
+    lengths = list(tiles.shape[1:])
+    lengths[dim] *= tiles.shape[0]
+    return jnp.moveaxis(tiles, 0, dim).reshape(lengths)
+
+
+def doubled(x, axis):
+    peers, here = (lax.axis_size(axis), lax.axis_index(axis))
+    blocks, apart = (x[None], 1)
+    while apart < peers:
+        other = lax.ppermute(blocks, axis, [(i, i ^ apart) for i in range(peers)])
+        low = here & apart == 0
+        blocks = jnp.concatenate([jnp.where(low, blocks, other), jnp.where(low, other, blocks)])
+        apart *= 2
+    return blocks
+
+
+def gather_by_bits(x, axis, dim):
+    return joined_along(doubled(x, axis), dim)
 
 
 def dot_rows(former, latter):
@@ -210,7 +231,7 @@
         lax.all_gather(shift_one, "dp", axis=0, tiled=True),
         lax.all_gather(w_up, "dp", axis=0, tiled=True),
         lax.all_gather(b_up, "dp", axis=0, tiled=True),
-        lax.all_gather(w_down, "dp", axis=0, tiled=True),
+        gather_by_bits(w_down, "dp", 0),
         lax.all_gather(b_down, "dp", axis=0, tiled=True),
         lax.all_gather(gain_two, "dp", axis=0, tiled=True),
         lax.all_gather(shift_two, "dp", axis=0, tiled=True),

time: 835 us -> 1100 us (1.32)
  blocking collectives: 180 us -> 515 us
  waiting for transfers between devices: 408 us -> 292 us
  other arithmetic: 25.5 us -> 53.4 us
  matrix products: 121 us -> 133 us
    all_gather x1, blocking collectives: 8.8 us -> 227 us  [local(): lax.all_gather(gain_one, 'dp', axis=0, tiled=True)]
    all_gather x1, blocking collectives: 10.3 us -> 85.6 us  [local(): lax.all_gather(b_query, 'dp', axis=0, tiled=True)]
    all_gather x1, waiting for transfers between devices: 59.7 us -> 0.01 us  [local(): lax.all_gather(w_down, 'dp', axis=0, tiled=True)]
    all_gather x1, blocking collectives: 9.57 us -> 61.5 us  [local(): lax.all_gather(b_out, 'dp', axis=0, tiled=True)]
    all_gather x1, waiting for transfers between devices: 22.6 us -> 0.01 us  [local(): lax.all_gather(w_key, 'dp', axis=0, tiled=True)]
    all_gather x1, waiting for transfers between devices: 16.8 us -> 0.01 us  [local(): lax.all_gather(w_value, 'dp', axis=0, tiled=True)]
    concatenate x0 -> x3, other arithmetic: none -> 13.2 us  [doubled(): jnp.concatenate([jnp.where(low, blocks, other), jnp.where(low, other, blo...]
    all_gather x1, waiting for transfers between devices: 12.3 us -> 0.01 us  [local(): lax.all_gather(w_query, 'dp', axis=0, tiled=True)]
  transfers between devices with their start and end apart: 18 -> 21, of which waited for: 11 -> 9; matrix products, arithmetic and copies ran while one was open for 15% -> 17% of each run, Pallas kernels for 0% -> 0%
where the time goes in v1:
time: 1100 us
  blocking collectives  515 us (47%)
  waiting for transfers between devices  292 us (27%)
  matrix products  133 us (12%)
  local copies, waits for them, and re-layouts  64.6 us (6%)
  other arithmetic  53.4 us (5%)
  starting transfers between devices  24.6 us (2%)
  between operations  16.2 us (1%)
    all_gather x1, blocking collectives, local(): lax.all_gather(gain_one, 'dp', axis=0, tiled=True)  227 us
    reduce_scatter x1, waiting for transfers between devices, local(): lax.psum_scatter(grad_w_up.astype(jnp.bfloat16), 'dp', scatter_dimension=...  90.5 us
    reduce_scatter x1, waiting for transfers between devices, local(): lax.psum_scatter(grad_w_down.astype(jnp.bfloat16), 'dp', scatter_dimensio...  90.2 us
    all_gather x1, blocking collectives, local(): lax.all_gather(b_query, 'dp', axis=0, tiled=True)  85.6 us
    all_gather x1, blocking collectives, local(): lax.all_gather(b_out, 'dp', axis=0, tiled=True)  61.5 us
    dot_general x7, matrix products, dot_rows(): return jnp.dot(former, latter, preferred_element_type=jnp.float32)  43.7 us
    psum x1, waiting for transfers between devices, local(): lax.psum(owned_grads[0].astype(jnp.bfloat16), 'seq').astype(jnp.float32)  38.4 us
    reduce_scatter x1, waiting for transfers between devices, local(): lax.psum_scatter(grad_w_out.astype(jnp.bfloat16), 'dp', scatter_dimension...  35.4 us
  transfers between devices with their start and end apart: 21, of which 9 were waited for; matrix products, arithmetic and copies ran while one was open for 17% of the time, Pallas kernels for 0%

profile of v1, /device:TPU:0, one launch (start us, length us, event | category | flops | bytes accessed | tf_op | source)
XLA Modules:
  0.0 1098.6 jit_solution(296451868258220752)
XLA Ops:
  20.5 85.6 %all-gather.1 = bf16[8,1,128]{2,1,0:T(2,128)(2,1)S(1)} all-gather(bf16[1,1,128]{2,1,0:T(2,128)(2,1)S(1)} %bitcast.213), channel_id=1, replica_groups=mesh['dp'=8,'seq'=4] {'dp'}, dimensions={0}, use_global_device_ids=true | all-gather | bytes 2304 | tf_op jit(solution)/shard_map/all_gather | solution.py:226
  110.1 3.7 all-to-all-start.1
  113.7 8.6 all-gather
  128.0 4.2 all-to-all-start.2
  132.2 3.5 broadcast_select_fusion.3
  139.9 5.8 all-to-all-done.2
  145.8 4.5 all-to-all-start
  150.3 4.1 pad_maximum_fusion.1
  163.2 7.5 multiply_reduce_fusion.1
  175.2 7.0 fusion
  183.6 3.6 fusion.20
  189.7 4.2 all-to-all-start.3
  193.9 61.5 %all-gather.2 = bf16[8,1,128]{2,1,0:T(2,128)(2,1)S(1)} all-gather(bf16[1,1,128]{2,1,0:T(2,128)(2,1)S(1)} %bitcast.215), channel_id=1, replica_groups=mesh['dp'=8,'seq'=4] {'dp'}, dimensions={0}, use_global_device_ids=true | all-gather | bytes 2304 | tf_op jit(solution)/shard_map/all_gather | solution.py:229
  255.4 226.6 %all-gather.3 = bf16[8,1,128]{2,1,0:T(2,128)(2,1)S(1)} all-gather(bf16[1,1,128]{2,1,0:T(2,128)(2,1)S(1)} %bitcast.216), channel_id=1, replica_groups=mesh['dp'=8,'seq'=4] {'dp'}, dimensions={0}, use_global_device_ids=true | all-gather | bytes 2304 | tf_op jit(solution)/shard_map/all_gather | solution.py:230
  482.0 8.6 all-gather.4
  490.7 12.7 %all-gather.5 = bf16[8,1,512]{2,1,0:T(2,128)(2,1)S(1)} all-gather(bf16[1,1,512]{2,1,0:T(2,128)(2,1)S(1)} %reshape.242), channel_id=1, replica_groups=mesh['dp'=8,'seq'=4] {'dp'}, dimensions={0}, use_global_device_ids=true | all-gather | bytes 9216 | tf_op jit(solution)/shard_map/all_gather | solution.py:233
  503.4 9.1 all-gather.6
  512.6 9.6 all-gather.7
  522.1 9.1 all-gather.8
  536.8 5.7 broadcast_select_fusion.1
  542.5 7.6 pad_maximum_fusion
  550.1 21.6 %multiply_convert_fusion.1 = (bf16[384,4096]{1,0:T(8,128)(2,1)S(1)}, f32[384,4096]{1,0:T(8,128)}, f32[384,4096]{1,0:T(8,128)}) fusion(f32[4096]{0:T(1024)S(1)} %bitcast.192, bf16[1024,4096]{1,0:T(8,128)(2,1)} %all-gather.24.cloned.1.call-done, f32[384,1024]{1,0:T(8,128)S(1)} %copy-done.12, f32[1024]{0:T(1024)S(1)} %bitcast.204, f32[1024]{0:T(1024)S(1)} %bitcast.193, ...), kind=kOutput, calls=%fused_computation.16 | convolution fusion | flops 3327000576 | bytes 25717760 | tf_op jit(solution)/shard_map/dot_general | solution.py:32
  571.8 3.6 fusion.36
  576.5 7.0 fusion.35
  586.9 13.3 %fusion.29 = (bf16[4096]{0:T(1024)(128)(2,1)S(1)}, bf16[384,4096]{1,0:T(8,128)(2,1)S(1)}) fusion(f32[384,4096]{1,0:T(8,128)} %get-tuple-element.125, f32[384,4096]{1,0:T(8,128)} %get-tuple-element.137, bf16[384,1024]{1,0:T(8,128)(2,1)S(1)} %get-tuple-element.115, bf16[4096,1024]{1,0:T(8,128)(2,1)} %all-gather.26.cloned.1.call-done), kind=kOutput, calls=%fused_computation.96 | convolution fusion | flops 3244814336 | bytes 24911872 | tf_op jit(solution)/shard_map/dot_general | solution.py:42
  600.2 4.0 multiply_reduce_fusion.2
  608.4 4.0 all-to-all-start.4
  612.3 14.1 %all-to-all-done.4 = bf16[3,128,1024]{1,0,2:T(4,128)(2,1)S(1)} async-done(((bf16[3,128,1024]{1,0,2:T(4,128)(2,1)}), bf16[3,128,1024]{1,0,2:T(4,128)(2,1)S(1)}, u32[]{:S(2)}, u32[]{:S(2)}) %all-to-all-start.4) | async-done | bytes 786464 | tf_op jit(solution)/shard_map/all_to_all | solution.py:317
  627.5 7.7 fusion.17
  636.8 16.5 %all_to_all.140 = bf16[3,512,256]{2,0,1:T(4,128)(2,1)S(1)} all-to-all(bf16[3,512,256]{2,0,1:T(4,128)(2,1)S(1)} %copy.96), channel_id=1, replica_groups=mesh['dp'=8,'seq'=4] {'seq'}, dimensions={1} | all-to-all | bytes 1572864 | tf_op jit(solution)/shard_map/all_to_all | solution.py:322
  657.8 3.9 copy.110
  661.8 6.7 multiply_reduce_fusion
  668.5 6.9 multiply_convert_fusion
  680.7 15.6 %all_to_all.141 = bf16[3,512,256]{2,0,1:T(4,128)(2,1)S(1)} all-to-all(bf16[3,512,256]{2,0,1:T(4,128)(2,1)} %copy.88), channel_id=1, replica_groups=mesh['dp'=8,'seq'=4] {'seq'}, dimensions={1} | all-to-all | bytes 1572864 | tf_op jit(solution)/shard_map/all_to_all | solution.py:320
  700.8 4.0 copy.106
  704.9 5.8 multiply_convert_fusion.2
  712.9 14.8 %all_to_all.142 = bf16[3,512,256]{2,0,1:T(4,128)(2,1)S(1)} all-to-all(bf16[3,512,256]{2,0,1:T(4,128)(2,1)} %copy.92), channel_id=1, replica_groups=mesh['dp'=8,'seq'=4] {'seq'}, dimensions={1} | all-to-all | bytes 1572864 | tf_op jit(solution)/shard_map/all_to_all | solution.py:321
  732.2 4.0 copy.108
  736.3 3.8 convolution_convert_fusion.2
  740.1 10.3 convolution_convert_fusion.1
  751.6 8.7 convolution_convert_fusion
  764.1 10.9 reduce-scatter.21.cloned.1.call-done
  776.8 35.4 %reduce-scatter.13.cloned.1.call-done = bf16[128,1024]{1,0:T(8,128)(2,1)} async-done(((bf16[1024,1024]{1,0:T(8,128)(2,1)}), bf16[128,1024]{1,0:T(8,128)(2,1)}) %reduce-scatter.13.cloned.1.call-update) | async-done | bytes 262160 | tf_op jit(solution)/shard_map/reduce_scatter | solution.py:355
  812.2 90.5 %reduce-scatter.15.cloned.1.call-done = bf16[128,4096]{1,0:T(8,128)(2,1)} async-done(((bf16[1024,4096]{1,0:T(8,128)(2,1)}), bf16[128,4096]{1,0:T(8,128)(2,1)}) %reduce-scatter.15.cloned.1.call-update) | async-done | bytes 1048592 | tf_op jit(solution)/shard_map/reduce_scatter | solution.py:367
  902.7 90.2 %reduce-scatter.17.cloned.1.call-done = bf16[512,1024]{1,0:T(8,128)(2,1)} async-done(((bf16[4096,1024]{1,0:T(8,128)(2,1)}), bf16[512,1024]{1,0:T(8,128)(2,1)}) %reduce-scatter.17.cloned.1.call-update) | async-done | bytes 1048592 | tf_op jit(solution)/shard_map/reduce_scatter | solution.py:373
  996.4 26.1 %all-reduce.9 = (bf16[1024]{0:T(1024)(128)(2,1)S(1)}, bf16[1024]{0:T(1024)(128)(2,1)S(1)}, bf16[1024]{0:T(1024)(128)(2,1)S(1)}, bf16[1024]{0:T(1024)(128)(2,1)S(...) all-reduce(bf16[1024]{0:T(1024)(128)(2,1)S(1)} %bitcast.203, ...), channel_id=5, replica_groups=mesh['dp'=8,'seq'=4] {'dp'}, use_global_device_ids=true, to_apply=%region_20.21.clone | all-reduce | flops 12288 | bytes 49152
  1023.2 10.4 all-reduce.10
  1045.3 38.4 %all-reduce.14.cloned.1.call-done = (bf16[128,1024]{0,1:T(8,128)(2,1)}, bf16[128,1024]{0,1:T(8,128)(2,1)}, bf16[128,1024]{0,1:T(8,128)(2,1)}, bf16[128,1024]{1,0...) async-done(((bf16[128,1024]{0,1:T(8,128)(2,1)}, bf16[128,1024]{0,1:T(8,128)(2,1)}, bf16[128,1024]{0,1:T(8,128)(2,1)}, bf16[128,1024]{1,0:T(8,128)(2,1)}, ...) | async-done | bytes 3145744 | tf_op jit(solution)/shard_map/psum | solution.py:387
  (256 shorter events, 111.3 us)
Async XLA Ops:
  7.2 98.9 %all-gather.18.cloned.1.call-start = ((), (), s32[]{:S(2)}) async-start(), calls=%async_computation.15 | async-start | bytes 2359296 | tf_op jit(solution)/shard_map/all_gather | solution.py:223
  7.9 114.5 %all-gather.20.cloned.1.call-start = ((), (), s32[]{:S(2)}) async-start(), calls=%async_computation.16 | async-start | bytes 2359296 | tf_op jit(solution)/shard_map/all_gather | solution.py:224
  8.7 127.0 %all-gather.16.cloned.1.call-start = ((), (), s32[]{:S(2)}) async-start(), calls=%async_computation.14 | async-start | bytes 2359296 | tf_op jit(solution)/shard_map/all_gather | solution.py:225
  9.4 522.8 %all-gather.22.cloned.1.call-start = ((), (), s32[]{:S(2)}) async-start(), calls=%async_computation.17 | async-start | bytes 2359296 | tf_op jit(solution)/shard_map/all_gather | solution.py:228
  10.0 540.1 %all-gather.24.cloned.1.call-start = ((), (), s32[]{:S(2)}) async-start(), calls=%async_computation.18 | async-start | bytes 9437184 | tf_op jit(solution)/shard_map/all_gather | solution.py:232
  10.6 565.9 %all-gather.26.cloned.1.call-start = ((), (), s32[]{:S(2)}) async-start(), calls=%async_computation.19 | async-start | bytes 9437184 | tf_op jit(solution)/shard_map/all_gather | solution.py:253
  10.6 3.0 collective-permute-start
  15.0 5.4 copy-start.35
  15.0 91.0 %copy-start.45 = (bf16[3,128,1024]{2,1,0:T(8,128)(2,1)S(1)}, bf16[3,128,1024]{2,1,0:T(8,128)(2,1)}, u32[]{:S(2)}) copy-start(bf16[3,128,1024]{2,1,0:T(8,128)(2,1)} %param.17) | copy-start | bytes 2359300
  17.5 114.7 %collective-permute-start.1 = (bf16[2,512,1024]{2,1,0:T(8,128)(2,1)}, bf16[2,512,1024]{2,1,0:T(8,128)(2,1)}, u32[]{:S(2)}, u32[]{:S(2)}) collective-permute-start(bf16[2,512,1024]{2,1,0:T(8,128)(2,1)} %pad_maximum_fusion.2), channel_id=1, source_target_pairs={{0,8},{4,12},{8,0},{12,4},{16,24},{20,28},{24,16},{28,20},{1,9},{5... | collective-permute-start | bytes 6291464 | tf_op jit(solution)/shard_map/ppermute | solution.py:20
  110.1 17.9 %all-to-all-start.1 = ((bf16[3,128,1024]{1,0,2:T(4,128)(2,1)}), bf16[3,128,1024]{1,0,2:T(4,128)(2,1)S(1)}, u32[]{:S(2)}, u32[]{:S(2)}) async-start(bf16[3,128,1024]{1,0,2:T(4,128)(2,1)} %copy.77), calls=%async_computation.1 | async-start | bytes 2097152 | tf_op jit(solution)/shard_map/all_to_all | solution.py:170
  128.0 17.8 %all-to-all-start.2 = ((bf16[3,128,1024]{1,0,2:T(4,128)(2,1)}), bf16[3,128,1024]{1,0,2:T(4,128)(2,1)}, u32[]{:S(2)}, u32[]{:S(2)}) async-start(bf16[3,128,1024]{1,0,2:T(4,128)(2,1)} %copy.79), calls=%async_computation.2 | async-start | bytes 2097152 | tf_op jit(solution)/shard_map/all_to_all | solution.py:171
  145.8 24.9 %all-to-all-start = ((bf16[3,128,1024]{1,0,2:T(4,128)(2,1)}), bf16[3,128,1024]{1,0,2:T(4,128)(2,1)}, u32[]{:S(2)}, u32[]{:S(2)}) async-start(bf16[3,128,1024]{1,0,2:T(4,128)(2,1)} %copy.75), calls=%async_computation | async-start | bytes 2097152 | tf_op jit(solution)/shard_map/all_to_all | solution.py:172
  154.4 382.4 %collective-permute-start.2 = (bf16[4,512,1024]{2,1,0:T(8,128)(2,1)}, bf16[4,512,1024]{2,1,0:T(8,128)(2,1)}, u32[]{:S(2)}, u32[]{:S(2)}) collective-permute-start(bf16[4,512,1024]{2,1,0:T(8,128)(2,1)} %pad_maximum_fusion.1), channel_id=1, source_target_pairs={{0,16},{4,20},{8,24},{12,28},{16,0},{20,4},{24,8},{28,12},{1,17},{... | collective-permute-start | bytes 12582920 | tf_op jit(solution)/shard_map/ppermute | solution.py:20
  157.7 13.0 %copy-start.4 = (bf16[3,512,4,64]{1,3,2,0:T(8,128)(2,1)}, bf16[3,512,4,64]{1,3,2,0:T(8,128)(2,1)S(1)}, u32[]{:S(2)}) copy-start(bf16[3,512,4,64]{1,3,2,0:T(8,128)(2,1)S(1)} %reshape.215) | copy-start | bytes 2359300
  175.2 7.0 copy-start.17
  175.2 8.4 copy-start
  187.2 6.7 copy-start.37
  187.2 68.1 %copy-start.38 = (bf16[128]{0:T(256)(128)(2,1)S(1)}, bf16[128]{0:T(256)(128)(2,1)}, u32[]{:S(2)}) copy-start(bf16[128]{0:T(256)(128)(2,1)} %param.25) | copy-start | bytes 772
  187.2 294.8 %copy-start.39 = (bf16[128]{0:T(256)(128)(2,1)S(1)}, bf16[128]{0:T(256)(128)(2,1)}, u32[]{:S(2)}) copy-start(bf16[128]{0:T(256)(128)(2,1)} %param.26) | copy-start | bytes 772
  187.2 303.4 %copy-start.34 = (bf16[512]{0:T(512)(128)(2,1)S(1)}, bf16[512]{0:T(512)(128)(2,1)}, u32[]{:S(2)}) copy-start(bf16[512]{0:T(512)(128)(2,1)} %param.28) | copy-start | bytes 3076
  187.2 316.2 %copy-start.40 = (bf16[128]{0:T(256)(128)(2,1)S(1)}, bf16[128]{0:T(256)(128)(2,1)}, u32[]{:S(2)}) copy-start(bf16[128]{0:T(256)(128)(2,1)} %param.30) | copy-start | bytes 772
  187.3 325.3 %copy-start.41 = (bf16[128]{0:T(256)(128)(2,1)S(1)}, bf16[128]{0:T(256)(128)(2,1)}, u32[]{:S(2)}) copy-start(bf16[128]{0:T(256)(128)(2,1)} %param.31) | copy-start | bytes 772
  187.3 334.9 %copy-start.42 = (bf16[128]{0:T(256)(128)(2,1)S(1)}, bf16[128]{0:T(256)(128)(2,1)}, u32[]{:S(2)}) copy-start(bf16[128]{0:T(256)(128)(2,1)} %param.32) | copy-start | bytes 772
  189.7 341.6 %all-to-all-start.3 = ((bf16[3,512,256]{2,0,1:T(4,128)(2,1)}), bf16[3,512,256]{2,0,1:T(4,128)(2,1)S(1)}, u32[]{:S(2)}, u32[]{:S(2)}) async-start(bf16[3,512,256]{2,0,1:T(4,128)(2,1)} %copy.82), calls=%async_computation.3 | async-start | bytes 2097152 | tf_op jit(solution)/shard_map/all_to_all | solution.py:175
  542.5 7.6 copy-start.12
  550.1 21.7 %copy-start.6 = (bf16[8,512,1024]{2,1,0:T(8,128)(2,1)S(1)}, bf16[8,512,1024]{2,1,0:T(8,128)(2,1)}, u32[]{:S(2)}) copy-start(bf16[8,512,1024]{2,1,0:T(8,128)(2,1)} %pad_maximum_fusion) | copy-start | bytes 25165828
  576.5 7.4 copy-start.9
  585.0 15.2 %slice-start = ((s8[8388608]{0:T(1024)(128)(4,1)}), s8[4194304]{0:T(1024)(128)(4,1)S(1)}, s32[]{:S(2)}) async-start(s8[8388608]{0:T(1024)(128)(4,1)} %bitcast.221), calls=%async_computation.27 | async-start | bytes 8388608
  586.8 13.4 %copy-start.27 = (bf16[384,1024]{1,0:T(8,128)(2,1)}, bf16[384,1024]{1,0:T(8,128)(2,1)S(1)}, u32[]{:S(2)}) copy-start(bf16[384,1024]{1,0:T(8,128)(2,1)S(1)} %get-tuple-element.115) | copy-start | bytes 2359300
  586.8 13.4 %slice-start.1 = ((s8[8388608]{0:T(1024)(128)(4,1)}), s8[4194304]{0:T(1024)(128)(4,1)S(1)}, s32[]{:S(2)}) async-start(s8[8388608]{0:T(1024)(128)(4,1)} %bitcast.221), calls=%async_computation.28 | async-start | bytes 8388608
  608.4 18.1 %all-to-all-start.4 = ((bf16[3,128,1024]{1,0,2:T(4,128)(2,1)}), bf16[3,128,1024]{1,0,2:T(4,128)(2,1)S(1)}, u32[]{:S(2)}, u32[]{:S(2)}) async-start(bf16[3,128,1024]{1,0,2:T(4,128)(2,1)} %copy.85), calls=%async_computation.4 | async-start | bytes 2097152 | tf_op jit(solution)/shard_map/all_to_all | solution.py:317
  612.3 148.1 %reduce-scatter.23.cloned.1.call-start = ((), (), s32[]{:S(2)}) async-start(), calls=%async_computation.25 | async-start | bytes 2359296
  636.8 18.4 %copy-start.46 = (bf16[3,128,1024]{2,1,0:T(8,128)(2,1)S(1)}, bf16[3,128,1024]{2,1,0:T(8,128)(2,1)}, u32[]{:S(2)}) copy-start(bf16[3,128,1024]{2,1,0:T(8,128)(2,1)} %param.17) | copy-start | bytes 2359300
  661.8 100.5 %reduce-scatter.19.cloned.1.call-start = ((), (), s32[]{:S(2)}) async-start(), calls=%async_computation.23 | async-start | bytes 2359296
  668.5 6.9 copy-start.10
  680.7 17.4 %copy-start.47 = (bf16[3,128,1024]{2,1,0:T(8,128)(2,1)S(1)}, bf16[3,128,1024]{2,1,0:T(8,128)(2,1)}, u32[]{:S(2)}) copy-start(bf16[3,128,1024]{2,1,0:T(8,128)(2,1)} %param.17) | copy-start | bytes 2359300
  704.8 70.2 %reduce-scatter.21.cloned.1.call-start = ((), (), s32[]{:S(2)}) async-start(), calls=%async_computation.24 | async-start | bytes 2359296
  712.9 16.7 %copy-start.48 = (bf16[3,128,1024]{2,1,0:T(8,128)(2,1)S(1)}, bf16[3,128,1024]{2,1,0:T(8,128)(2,1)}, u32[]{:S(2)}) copy-start(bf16[3,128,1024]{2,1,0:T(8,128)(2,1)} %param.17) | copy-start | bytes 2359300
  736.3 75.9 %reduce-scatter.13.cloned.1.call-start = ((), (), s32[]{:S(2)}) async-start(), calls=%async_computation.20 | async-start | bytes 2359296 | tf_op jit(solution)/shard_map/reduce_scatter | solution.py:355
  740.1 162.6 %reduce-scatter.15.cloned.1.call-start = ((), (), s32[]{:S(2)}) async-start(), calls=%async_computation.21 | async-start | bytes 9437184 | tf_op jit(solution)/shard_map/reduce_scatter | solution.py:367
  750.5 242.4 %reduce-scatter.17.cloned.1.call-start = ((), (), s32[]{:S(2)}) async-start(), calls=%async_computation.22 | async-start | bytes 9437184 | tf_op jit(solution)/shard_map/reduce_scatter | solution.py:373
  760.4 233.8 %copy-start.49 = (u32[32]{0:T(128)S(1)}, u32[32]{0:T(128)}, u32[]{:S(2)}) copy-start(u32[32]{0:T(128)} %constant.109) | copy-start | bytes 388
  760.4 235.8 %copy-start.8 = (bf16[3,512,256]{2,1,0:T(8,128)(2,1)S(1)}, bf16[3,512,256]{2,1,0:T(8,128)(2,1)}, u32[]{:S(2)}) copy-start(bf16[3,512,256]{2,1,0:T(8,128)(2,1)} %copy-done.7) | copy-start | bytes 2359300
  760.4 323.4 %all-reduce.14.cloned.1.call-start = ((), (), s32[]{:S(2)}) async-start(), calls=%async_computation.26 | async-start | bytes 6291456 | tf_op jit(solution)/shard_map/psum | solution.py:387
  996.2 45.0 %copy-start.26 = (bf16[48,8,4,256]{3,1,2,0:T(8,128)(2,1)S(1)}, bf16[48,8,4,256]{3,1,2,0:T(8,128)(2,1)}, u32[]{:S(2)}) copy-start(bf16[48,8,4,256]{3,1,2,0:T(8,128)(2,1)} %copy-done.25) | copy-start | bytes 2359300
  1033.6 7.6 copy-start.43
  1083.8 5.3 copy-start.32
  (27 other events, 70.1 us)
Sparse Core Ops, SparseCore 0:
  9.6 44.1 all-gather.17
  55.5 43.6 all-gather.19
  100.8 32.1 all-gather.15
  134.5 121.2 all-gather.21
  257.2 114.6 all-gather.23
  373.3 106.1 all-gather.25
  661.9 33.2 reduce-scatter.22
  704.9 33.4 reduce-scatter.18
  740.7 34.2 reduce-scatter.20
  777.7 34.4 reduce-scatter.12
  814.5 88.1 reduce-scatter.14
  904.9 87.9 reduce-scatter.16
  997.2 86.5 all-reduce.13
